TPU v7x, 512 devices: a whole 4x4x16 slice. The times are simulated.
512 devices in a mesh: gx: 64 (over y, z), ta: 8 (over x, core).
Axes of the slice: x: 4, y: 4, z: 16, core: 2. Of those that a mesh axis runs over, the one named last changes fastest.
Arguments:
- query_vecs: bfloat16 [256, 64, 5120], P('gx', None, 'ta'), may hold values from -32 to 32
- key_vecs: bfloat16 [256, 64, 5120], P('gx', None, 'ta'), may hold values from -6 to 6
- value_vecs: bfloat16 [256, 64, 5120], P('gx', None, 'ta'), may hold values from -6 to 6
- slot_map: int32 [16, 64], replicated, may hold values from 0 to 63, each once within a row
- edge_list: int32 [256, 2], replicated, may hold values from 0 to 63
- edge_types: int32 [256], replicated, may hold values from 0 to 2
- type_gain: float32 [2, 3, 5120], P(None, None, 'ta'), may hold values from 0.25 to 2
- norm_gain: float32 [2, 5120], P(None, 'ta'), may hold values from 0.5 to 2
- gate_proj: bfloat16 [2, 5120, 20480], P(None, 'ta', 'gx'), may hold values from -0.078125 to 0.078125
- up_proj: bfloat16 [2, 5120, 20480], P(None, 'ta', 'gx'), may hold values from -0.078125 to 0.078125
- down_proj: bfloat16 [2, 20480, 5120], P(None, 'gx', 'ta'), may hold values from -0.0390625 to 0.0390625
Outputs:
- node_states: bfloat16 [512, 5120], P('gx', 'ta')
All inputs are finite; a program needn't handle non-finite values.
Results may differ from a plain program's by a relative error of at most 0.04.
Values may be sent and summed in bfloat16 or wider, within the bound.
A program may use at most 64 MiB of HBM per device.

v0:
```python
import jax
import jax.numpy as jnp
from jax import lax
from jax.sharding import PartitionSpec as P

D = 5120
HEAD_DIM = 128
VENUES = 16
STEPS = 16
NODE_STEPS = 8
ROUNDS = 2
ETYPES = 3


def settle_rows(nodes, hidden, down_local, row_begin, rows_dev):
    summed = lax.psum_scatter(
        jnp.dot(hidden, down_local, preferred_element_type=jnp.float32),
        "gx",
        scatter_dimension=0,
        tiled=True,
    )
    base_rows = lax.dynamic_slice_in_dim(nodes, row_begin, rows_dev, 0)
    return (base_rows.astype(jnp.float32) + summed).astype(jnp.bfloat16)


def per_device(
    query_vecs,
    key_vecs,
    value_vecs,
    slot_map,
    edge_list,
    edge_types,
    type_gain,
    norm_gain,
    gate_proj,
    up_proj,
    down_proj,
):
    pairs_dev = query_vecs.shape[0]
    inst_total = query_vecs.shape[1]
    feat_width = query_vecs.shape[2]
    head_count = feat_width // HEAD_DIM
    gx_count = lax.axis_size("gx")
    inst_local = inst_total // gx_count
    score_scale = 1.0 / HEAD_DIM**0.5
    venue_idx = lax.axis_index("gx") * pairs_dev // STEPS
    slot_order = lax.dynamic_index_in_dim(slot_map, venue_idx, 0, keepdims=False)
    split_shape = (pairs_dev, gx_count, inst_local, feat_width)
    sorted_queries = jnp.take(query_vecs, slot_order, axis=1).reshape(split_shape)
    sorted_keys = jnp.take(key_vecs, slot_order, axis=1).reshape(split_shape)
    sorted_values = jnp.take(value_vecs, slot_order, axis=1).reshape(split_shape)
    query_steps = jnp.arange(VENUES * NODE_STEPS) % NODE_STEPS + (STEPS - NODE_STEPS)
    key_steps = jnp.arange(VENUES * STEPS) % STEPS
    allowed = key_steps[None, :] <= query_steps[:, None]
    queries = lax.all_to_all(sorted_queries, "gx", split_axis=1, concat_axis=0, tiled=True)
    keyset = lax.all_to_all(sorted_keys, "gx", split_axis=1, concat_axis=0, tiled=True)
    valueset = lax.all_to_all(sorted_values, "gx", split_axis=1, concat_axis=0, tiled=True)
    pair_total = queries.shape[0]
    item_count = queries.shape[2]
    queries = queries.reshape(VENUES, STEPS, item_count, head_count, HEAD_DIM)[
        :, STEPS - NODE_STEPS :
    ]
    queries = queries.reshape(VENUES * NODE_STEPS, item_count, head_count, HEAD_DIM)
    keyset = keyset.reshape(pair_total, item_count, head_count, HEAD_DIM)
    valueset = valueset.reshape(pair_total, item_count, head_count, HEAD_DIM)
    scores = (
        jnp.einsum("qnhd,knhd->nhqk", queries, keyset, preferred_element_type=jnp.float32)
        * score_scale
    )
    scores = jnp.where(allowed[None, None], scores, jnp.float32(-1e30))
    row_max = jnp.max(scores, axis=-1, keepdims=True)
    expd = jnp.exp(scores - row_max)
    probs = (expd / jnp.sum(expd, axis=-1, keepdims=True)).astype(jnp.bfloat16)
    attended = jnp.einsum("nhqk,knhd->nqhd", probs, valueset, preferred_element_type=jnp.float32)
    attended = attended.reshape(item_count, VENUES, NODE_STEPS, feat_width)
    pooled = jnp.mean(attended, axis=1).astype(jnp.bfloat16)
    own_rows = pooled.reshape(inst_local * NODE_STEPS, feat_width)
    rows_dev = own_rows.shape[0]
    row_begin = lax.axis_index("gx") * rows_dev
    nodes = lax.all_gather(own_rows, "gx", axis=0, tiled=True)
    row_total = nodes.shape[0]
    node_ids = jnp.arange(inst_total)
    type_ids = jnp.arange(ETYPES)
    at_source = (edge_list[:, 0][:, None] == node_ids[None, :]).astype(jnp.float32)
    at_target = (edge_list[:, 1][:, None] == node_ids[None, :]).astype(jnp.float32)
    of_type = (edge_types[:, None] == type_ids[None, :]).astype(jnp.float32)
    adjacency = jnp.einsum("et,ei,ej->tij", of_type, at_target, at_source)
    degree = jnp.maximum(jnp.sum(at_target, axis=0), 1.0)
    adj_rows = adjacency.reshape(ETYPES * inst_total, inst_total).astype(jnp.bfloat16)
    for layer_idx in range(ROUNDS):
        flat_nodes = nodes.reshape(inst_total, NODE_STEPS * feat_width)
        gathered = jnp.dot(adj_rows, flat_nodes, preferred_element_type=jnp.float32)
        gathered = gathered.reshape(ETYPES, inst_total, NODE_STEPS, feat_width)
        message = (
            jnp.sum(gathered * type_gain[layer_idx][:, None, None, :], axis=0)
            / degree[:, None, None]
        )
        pre_norm = nodes.astype(jnp.float32) + message.reshape(row_total, feat_width)
        squares = lax.psum(jnp.sum(pre_norm * pre_norm, axis=-1), "ta")
        row_scale = lax.rsqrt(squares / D + 1e-05)[:, None]
        normed = (pre_norm * row_scale * norm_gain[layer_idx][None, :]).astype(jnp.bfloat16)
        gate_part = jnp.dot(normed, gate_proj[layer_idx], preferred_element_type=jnp.float32)
        up_part = jnp.dot(normed, up_proj[layer_idx], preferred_element_type=jnp.float32)
        gate_sum, up_sum = (
            lax.psum(gate_part.astype(jnp.bfloat16), "ta").astype(jnp.float32),
            lax.psum(up_part.astype(jnp.bfloat16), "ta").astype(jnp.float32),
        )
        hidden = (jax.nn.silu(gate_sum) * up_sum).astype(jnp.bfloat16)
        down_local = down_proj[layer_idx]
        if layer_idx == ROUNDS - 1:
            own_rows = settle_rows(nodes, hidden, down_local, row_begin, rows_dev)
        else:
            own_rows = settle_rows(nodes, hidden, down_local, row_begin, rows_dev)
            nodes = lax.all_gather(own_rows, "gx", axis=0, tiled=True)
    return own_rows


def solution(mesh):
    placed = (
        P("gx", None, "ta"),
        P("gx", None, "ta"),
        P("gx", None, "ta"),
        P(),
        P(),
        P(),
        P(None, None, "ta"),
        P(None, "ta"),
        P(None, "ta", "gx"),
        P(None, "ta", "gx"),
        P(None, "gx", "ta"),
    )
    return jax.shard_map(
        per_device, mesh=mesh, in_specs=placed, out_specs=P("gx", "ta"), check_vma=False
    )
```

profile of v0, /device:TPU:2, one launch (start us, length us, event | category | flops | bytes accessed | tf_op | source)
XLA Modules:
  0.0 1049.3 jit_solution(5708310502350677954)
XLA Ops:
  6.5 0.7 compare_and_fusion
  7.5 1.6 gather_fusion
  9.1 1.6 gather_fusion.1
  10.8 1.6 gather_fusion.2
  12.5 1.0 copy.32
  13.5 18.9 %all-to-all-start.1 = ((bf16[4,64,1,640]{3,0,2,1:T(4,128)(2,1)}), bf16[4,64,1,640]{3,0,2,1:T(4,128)(2,1)S(1)}, u32[]{:S(2)}, u32[]{:S(2)}) async-start(bf16[4,64,1,640]{3,0,2,1:T(4,128)(2,1)} %copy.32), calls=%async_computation.1 | async-start | bytes 655360 | tf_op jit(solution)/shard_map/all_to_all | solution.py:55
  32.4 1.0 copy.34
  33.4 22.7 %all-to-all-done.1 = bf16[4,64,1,640]{3,0,2,1:T(4,128)(2,1)S(1)} async-done(((bf16[4,64,1,640]{3,0,2,1:T(4,128)(2,1)}), bf16[4,64,1,640]{3,0,2,1:T(4,128)(2,1)S(1)}, u32[]{:S(2)}, u32[]{:S(2)}) %all-to-all-start.1) | async-done | bytes 327712 | tf_op jit(solution)/shard_map/all_to_all | solution.py:55
  56.1 6.5 all-to-all-start.2
  62.6 1.0 copy.31
  64.0 21.6 %all-to-all-done.2 = bf16[4,64,1,640]{3,0,2,1:T(4,128)(2,1)S(1)} async-done(((bf16[4,64,1,640]{3,0,2,1:T(4,128)(2,1)}), bf16[4,64,1,640]{3,0,2,1:T(4,128)(2,1)S(1)}, u32[]{:S(2)}, u32[]{:S(2)}) %all-to-all-start.2) | async-done | bytes 327712 | tf_op jit(solution)/shard_map/all_to_all | solution.py:56
  85.6 6.6 all-to-all-start
  93.6 20.9 %all-to-all-done = bf16[4,64,1,640]{3,0,2,1:T(4,128)(2,1)S(1)} async-done(((bf16[4,64,1,640]{3,0,2,1:T(4,128)(2,1)}), bf16[4,64,1,640]{3,0,2,1:T(4,128)(2,1)S(1)}, u32[]{:S(2)}, u32[]{:S(2)}) %all-to-all-start) | async-done | bytes 327712 | tf_op jit(solution)/shard_map/all_to_all | solution.py:57
  114.6 1.4 convolution_bitcast_fusion
  116.4 99.8 %all_gather.6 = bf16[512,640]{1,0:T(8,128)(2,1)S(1)} all-gather(bf16[8,640]{1,0:T(8,128)(2,1)S(1)} %multiply_convert_fusion.2), channel_id=1, replica_groups=mesh['gx'=64,'ta'=8] {'gx'}, dimensions={0}, use_global_device_ids=true | all-gather | bytes 665600 | tf_op jit(solution)/shard_map/all_gather | solution.py:80
  217.2 0.9 multiply_reduce_fusion.3
  218.1 10.0 psum.42
  228.1 1.3 convolution_convert_fusion.3
  229.4 1.3 convolution_convert_fusion.2
  230.7 67.0 %all-reduce.15.cloned.1.call-done = (bf16[512,320]{0,1:T(8,128)(2,1)}, bf16[512,320]{0,1:T(8,128)(2,1)}) async-done(((bf16[512,320]{0,1:T(8,128)(2,1)}, bf16[512,320]{0,1:T(8,128)(2,1)}), (bf16[512,320]{0,1:T(8,128)(2,1)}, bf16[512,320]{0,1:T(8,128)(2,1)})) %all-reduce.15.cloned.1.call-update) | async-done | bytes 655376 | tf_op jit(solution)/shard_map/psum | solution.py:106
  297.7 2.9 fusion.23
  300.7 1.3 dynamic-slice
  302.6 275.2 %all-reduce.9.cloned.1.call-done = f32[512,640]{1,0:T(8,128)} async-done(((f32[512,640]{1,0:T(8,128)}), f32[512,640]{1,0:T(8,128)}) %all-reduce.9.cloned.1.call-update) | async-done | bytes 1310736
  578.6 98.7 %all_gather.7 = bf16[512,640]{1,0:T(8,128)(2,1)S(1)} all-gather(bf16[8,640]{1,0:T(8,128)(2,1)S(1)} %fusion.51), channel_id=1, replica_groups=mesh['gx'=64,'ta'=8] {'gx'}, dimensions={0}, use_global_device_ids=true | all-gather | bytes 665600 | tf_op jit(solution)/shard_map/all_gather | solution.py:114
  678.3 0.9 multiply_reduce_fusion.2
  679.2 10.0 psum.45
  689.2 1.3 convolution_convert_fusion.1
  690.5 1.2 convolution_convert_fusion
  691.8 69.7 %all-reduce.13.cloned.1.call-done = (bf16[512,320]{0,1:T(8,128)(2,1)}, bf16[512,320]{0,1:T(8,128)(2,1)}) async-done(((bf16[512,320]{0,1:T(8,128)(2,1)}, bf16[512,320]{0,1:T(8,128)(2,1)}), (bf16[512,320]{0,1:T(8,128)(2,1)}, bf16[512,320]{0,1:T(8,128)(2,1)})) %all-reduce.13.cloned.1.call-update) | async-done | bytes 655376 | tf_op jit(solution)/shard_map/psum | solution.py:106
  761.5 2.8 fusion.19
  764.3 277.2 %all-reduce.11.cloned.1.call-done = f32[512,640]{1,0:T(8,128)} async-done(((f32[512,640]{1,0:T(8,128)}), f32[512,640]{1,0:T(8,128)}) %all-reduce.11.cloned.1.call-update) | async-done | bytes 1310736
  1041.4 1.3 fusion.50
  (64 shorter events, 5.5 us)
Async XLA Ops:
  6.5 1.0 copy-start
  7.5 1.6 copy-start.1
  9.1 1.6 copy-start.2
  13.5 50.0 %copy-start.6 = (f32[2,3,640]{2,0,1:T(2,128)S(1)}, f32[2,3,640]{2,0,1:T(2,128)}, u32[]{:S(2)}) copy-start(f32[2,3,640]{2,0,1:T(2,128)} %param.19) | copy-start | bytes 46084
  13.5 50.1 %copy-start.8 = (s32[256,2]{0,1:T(2,128)S(1)}, s32[256,2]{0,1:T(2,128)}, u32[]{:S(2)}) copy-start(s32[256,2]{0,1:T(2,128)} %param.17) | copy-start | bytes 6148
  13.5 50.4 %copy-start.7 = (f32[2,640]{1,0:T(2,128)S(1)}, f32[2,640]{1,0:T(2,128)}, u32[]{:S(2)}) copy-start(f32[2,640]{1,0:T(2,128)} %param.20) | copy-start | bytes 15364
  13.5 42.6 %all-to-all-start.1 = ((bf16[4,64,1,640]{3,0,2,1:T(4,128)(2,1)}), bf16[4,64,1,640]{3,0,2,1:T(4,128)(2,1)S(1)}, u32[]{:S(2)}, u32[]{:S(2)}) async-start(bf16[4,64,1,640]{3,0,2,1:T(4,128)(2,1)} %copy.32), calls=%async_computation.1 | async-start | bytes 655360 | tf_op jit(solution)/shard_map/all_to_all | solution.py:55
  32.4 59.8 %copy-start.9 = (s32[256]{0:T(256)S(1)}, s32[256]{0:T(256)}, u32[]{:S(2)}) copy-start(s32[256]{0:T(256)} %param.18) | copy-start | bytes 3076
  56.1 29.5 %all-to-all-start.2 = ((bf16[4,64,1,640]{3,0,2,1:T(4,128)(2,1)}), bf16[4,64,1,640]{3,0,2,1:T(4,128)(2,1)S(1)}, u32[]{:S(2)}, u32[]{:S(2)}) async-start(bf16[4,64,1,640]{3,0,2,1:T(4,128)(2,1)} %copy.34), calls=%async_computation.2 | async-start | bytes 655360 | tf_op jit(solution)/shard_map/all_to_all | solution.py:56
  85.6 28.9 %all-to-all-start = ((bf16[4,64,1,640]{3,0,2,1:T(4,128)(2,1)}), bf16[4,64,1,640]{3,0,2,1:T(4,128)(2,1)S(1)}, u32[]{:S(2)}, u32[]{:S(2)}) async-start(bf16[4,64,1,640]{3,0,2,1:T(4,128)(2,1)} %copy.31), calls=%async_computation | async-start | bytes 655360 | tf_op jit(solution)/shard_map/all_to_all | solution.py:57
  92.1 205.6 %all-reduce.15.cloned.1.call-start = ((), (), s32[]{:S(2)}) async-start(), calls=%async_computation.6 | async-start | bytes 1310720 | tf_op jit(solution)/shard_map/psum | solution.py:106
  217.2 10.9 %copy-start.3 = (bf16[2,640,320]{1,2,0:T(8,128)(2,1)S(1)}, bf16[2,640,320]{1,2,0:T(8,128)(2,1)}, u32[]{:S(2)}) copy-start(bf16[2,640,320]{1,2,0:T(8,128)(2,1)} %param.21) | copy-start | bytes 2457604
  228.1 1.3 copy-start.4
  230.7 347.1 %all-reduce.9.cloned.1.call-start = ((), (), s32[]{:S(2)}) async-start(), calls=%async_computation.3 | async-start | bytes 2621440
  300.6 460.8 %all-reduce.13.cloned.1.call-start = ((), (), s32[]{:S(2)}) async-start(), calls=%async_computation.5 | async-start | bytes 1310720 | tf_op jit(solution)/shard_map/psum | solution.py:106
  689.2 1.3 copy-start.5
  690.5 71.0 %copy-start.10 = (bf16[2,320,640]{2,1,0:T(8,128)(2,1)S(1)}, bf16[2,320,640]{2,1,0:T(8,128)(2,1)}, u32[]{:S(2)}) copy-start(bf16[2,320,640]{2,1,0:T(8,128)(2,1)} %param.23) | copy-start | bytes 2457604
  691.7 349.7 %all-reduce.11.cloned.1.call-start = ((), (), s32[]{:S(2)}) async-start(), calls=%async_computation.4 | async-start | bytes 2621440
Sparse Core Ops, SparseCore 0:
  230.8 66.8 all-reduce.14
  301.1 276.7 all-reduce.8
  691.8 69.5 all-reduce.12
  764.6 276.7 all-reduce.10
where the time goes:
time: 1050 us
  waiting for transfers between devices  754 us (72%)
  blocking collectives  219 us (21%)
  starting transfers between devices  32.1 us (3%)
  matrix products  14.3 us (1%)
  between operations  14.1 us (1%)
  local copies, waits for them, and re-layouts  10.9 us (1%)
    unnamed x6, waiting for transfers between devices  552 us
    all_gather x2, blocking collectives, per_device(): nodes = lax.all_gather(own_rows, 'gx', axis=0, tiled=True)  199 us
    psum x2, waiting for transfers between devices, per_device(): lax.psum(up_part.astype(jnp.bfloat16), 'ta').astype(jnp.float32)  137 us
    all_to_all x1, waiting for transfers between devices, per_device(): lax.all_to_all(sorted_queries, 'gx', split_axis=1, concat_axis=0, tiled=T...  22.7 us
    all_to_all x1, waiting for transfers between devices, per_device(): lax.all_to_all(sorted_keys, 'gx', split_axis=1, concat_axis=0, tiled=True)  21.6 us
  transfers between devices with their start and end apart: 7, of which 7 were waited for; matrix products, arithmetic and copies ran while one was open for 0% of the time, Pallas kernels for 0%

commit v1 on v0

--- a/solution.py
+++ b/solution.py
@@ -103,7 +103,7 @@
         up_part = jnp.dot(normed, up_proj[layer_idx], preferred_element_type=jnp.float32)
         gate_sum, up_sum = (
             lax.psum(gate_part.astype(jnp.bfloat16), "ta").astype(jnp.float32),
-            lax.psum(up_part.astype(jnp.bfloat16), "ta").astype(jnp.float32),
+            jnp.sum(lax.all_gather(up_part.astype(jnp.bfloat16), "ta"), axis=0).astype(jnp.float32),
         )
         hidden = (jax.nn.silu(gate_sum) * up_sum).astype(jnp.bfloat16)
         down_local = down_proj[layer_idx]

time: 1050 us -> 1120 us (1.067)
  waiting for transfers between devices: 754 us -> 811 us
    all_gather x0 -> x2, waiting for transfers between devices: none -> 48.4 us  [per_device(): lax.all_gather(up_part.astype(jnp.bfloat16), 'ta')]
    unnamed x6 -> x8, waiting for transfers between devices: 552 us -> 553 us
  transfers between devices with their start and end apart: 7 -> 9, of which waited for: 7 -> 9; matrix products, arithmetic and copies ran while one was open for 0% -> 2% of each run, Pallas kernels for 0% -> 0%
where the time goes in v1:
time: 1120 us
  waiting for transfers between devices  811 us (72%)
  blocking collectives  219 us (20%)
  starting transfers between devices  32.4 us (3%)
  local copies, waits for them, and re-layouts  16.7 us (1%)
  matrix products  16 us (1%)
  between operations  14.5 us (1%)
    unnamed x8, waiting for transfers between devices  553 us
    all_gather x2, blocking collectives, per_device(): nodes = lax.all_gather(own_rows, 'gx', axis=0, tiled=True)  199 us
    psum x2, waiting for transfers between devices, per_device(): lax.psum(gate_part.astype(jnp.bfloat16), 'ta').astype(jnp.float32)  145 us
    all_gather x2, waiting for transfers between devices, per_device(): lax.all_gather(up_part.astype(jnp.bfloat16), 'ta')  48.4 us
    all_to_all x1, waiting for transfers between devices, per_device(): lax.all_to_all(sorted_queries, 'gx', split_axis=1, concat_axis=0, tiled=T...  22.7 us
  transfers between devices with their start and end apart: 9, of which 9 were waited for; matrix products, arithmetic and copies ran while one was open for 2% of the time, Pallas kernels for 0%

profile of v1, /device:TPU:2, one launch (start us, length us, event | category | flops | bytes accessed | tf_op | source)
XLA Modules:
  0.0 1118.1 jit_solution(7926662437978932111)
XLA Ops:
  7.5 1.6 gather_fusion
  9.1 1.6 gather_fusion.1
  10.8 1.6 gather_fusion.2
  13.5 18.9 %all-to-all-start.1 = ((bf16[4,64,1,640]{3,0,2,1:T(4,128)(2,1)}), bf16[4,64,1,640]{3,0,2,1:T(4,128)(2,1)S(1)}, u32[]{:S(2)}, u32[]{:S(2)}) async-start(bf16[4,64,1,640]{3,0,2,1:T(4,128)(2,1)} %copy.32), calls=%async_computation.1 | async-start | bytes 655360 | tf_op jit(solution)/shard_map/all_to_all | solution.py:55
  33.4 22.7 %all-to-all-done.1 = bf16[4,64,1,640]{3,0,2,1:T(4,128)(2,1)S(1)} async-done(((bf16[4,64,1,640]{3,0,2,1:T(4,128)(2,1)}), bf16[4,64,1,640]{3,0,2,1:T(4,128)(2,1)S(1)}, u32[]{:S(2)}, u32[]{:S(2)}) %all-to-all-start.1) | async-done | bytes 327712 | tf_op jit(solution)/shard_map/all_to_all | solution.py:55
  56.1 6.5 all-to-all-start.2
  64.0 21.6 %all-to-all-done.2 = bf16[4,64,1,640]{3,0,2,1:T(4,128)(2,1)S(1)} async-done(((bf16[4,64,1,640]{3,0,2,1:T(4,128)(2,1)}), bf16[4,64,1,640]{3,0,2,1:T(4,128)(2,1)S(1)}, u32[]{:S(2)}, u32[]{:S(2)}) %all-to-all-start.2) | async-done | bytes 327712 | tf_op jit(solution)/shard_map/all_to_all | solution.py:56
  85.6 6.6 all-to-all-start
  93.6 20.9 %all-to-all-done = bf16[4,64,1,640]{3,0,2,1:T(4,128)(2,1)S(1)} async-done(((bf16[4,64,1,640]{3,0,2,1:T(4,128)(2,1)}), bf16[4,64,1,640]{3,0,2,1:T(4,128)(2,1)S(1)}, u32[]{:S(2)}, u32[]{:S(2)}) %all-to-all-start) | async-done | bytes 327712 | tf_op jit(solution)/shard_map/all_to_all | solution.py:57
  114.6 1.4 convolution_bitcast_fusion
  116.4 99.8 %all_gather.18 = bf16[512,640]{1,0:T(8,128)(2,1)S(1)} all-gather(bf16[8,640]{1,0:T(8,128)(2,1)S(1)} %multiply_convert_fusion.2), channel_id=1, replica_groups=mesh['gx'=64,'ta'=8] {'gx'}, dimensions={0}, use_global_device_ids=true | all-gather | bytes 665600 | tf_op jit(solution)/shard_map/all_gather | solution.py:80
  218.1 10.0 psum.28
  228.1 1.3 convolution_convert_fusion.2
  229.5 2.3 convolution_convert_fusion.3
  231.8 22.9 %all-gather.5.cloned.1.call-done = bf16[4096,320]{0,1:T(8,128)(2,1)} async-done(((bf16[512,320]{0,1:T(8,128)(2,1)}), bf16[4096,320]{0,1:T(8,128)(2,1)}) %all-gather.5.cloned.1.call-update) | async-done | bytes 2621456 | tf_op jit(solution)/shard_map/all_gather | solution.py:106
  254.8 2.9 copy.47
  257.7 1.9 bitcast_reduce_fusion.1
  259.6 72.4 %all-reduce.7.cloned.1.call-done = bf16[512,320]{0,1:T(8,128)(2,1)} async-done(((bf16[512,320]{0,1:T(8,128)(2,1)}), bf16[512,320]{0,1:T(8,128)(2,1)}) %all-reduce.7.cloned.1.call-update) | async-done | bytes 327696 | tf_op jit(solution)/shard_map/psum | solution.py:105
  332.0 2.7 fusion.23
  334.8 1.3 dynamic-slice
  336.7 275.6 %all-reduce.11.cloned.1.call-done = f32[512,640]{1,0:T(8,128)} async-done(((f32[512,640]{1,0:T(8,128)}), f32[512,640]{1,0:T(8,128)}) %all-reduce.11.cloned.1.call-update) | async-done | bytes 1310736
  613.1 98.7 %all_gather.21 = bf16[512,640]{1,0:T(8,128)(2,1)S(1)} all-gather(bf16[8,640]{1,0:T(8,128)(2,1)S(1)} %fusion.51), channel_id=1, replica_groups=mesh['gx'=64,'ta'=8] {'gx'}, dimensions={0}, use_global_device_ids=true | all-gather | bytes 665600 | tf_op jit(solution)/shard_map/all_gather | solution.py:114
  713.6 10.0 psum.30
  723.7 1.3 convolution_convert_fusion
  725.0 2.3 convolution_convert_fusion.1
  727.6 25.4 %all-gather.7.cloned.1.call-done = bf16[4096,320]{0,1:T(8,128)(2,1)} async-done(((bf16[512,320]{0,1:T(8,128)(2,1)}), bf16[4096,320]{0,1:T(8,128)(2,1)}) %all-gather.7.cloned.1.call-update) | async-done | bytes 2621456 | tf_op jit(solution)/shard_map/all_gather | solution.py:106
  753.0 2.9 copy.48
  755.9 1.9 bitcast_reduce_fusion
  757.9 72.3 %all-reduce.9.cloned.1.call-done = bf16[512,320]{0,1:T(8,128)(2,1)} async-done(((bf16[512,320]{0,1:T(8,128)(2,1)}), bf16[512,320]{0,1:T(8,128)(2,1)}) %all-reduce.9.cloned.1.call-update) | async-done | bytes 327696 | tf_op jit(solution)/shard_map/psum | solution.py:105
  830.2 2.7 fusion.19
  832.9 277.1 %all-reduce.13.cloned.1.call-done = f32[512,640]{1,0:T(8,128)} async-done(((f32[512,640]{1,0:T(8,128)}), f32[512,640]{1,0:T(8,128)}) %all-reduce.13.cloned.1.call-update) | async-done | bytes 1310736
  1110.0 1.3 fusion.50
  (72 shorter events, 11.4 us)
Async XLA Ops:
  6.5 1.0 copy-start
  7.5 1.6 copy-start.1
  9.1 1.6 copy-start.2
  13.5 50.0 %copy-start.4 = (f32[2,3,640]{2,0,1:T(2,128)S(1)}, f32[2,3,640]{2,0,1:T(2,128)}, u32[]{:S(2)}) copy-start(f32[2,3,640]{2,0,1:T(2,128)} %param.19) | copy-start | bytes 46084
  13.5 50.1 %copy-start.6 = (s32[256,2]{0,1:T(2,128)S(1)}, s32[256,2]{0,1:T(2,128)}, u32[]{:S(2)}) copy-start(s32[256,2]{0,1:T(2,128)} %param.17) | copy-start | bytes 6148
  13.5 50.4 %copy-start.5 = (f32[2,640]{1,0:T(2,128)S(1)}, f32[2,640]{1,0:T(2,128)}, u32[]{:S(2)}) copy-start(f32[2,640]{1,0:T(2,128)} %param.20) | copy-start | bytes 15364
  13.5 42.6 %all-to-all-start.1 = ((bf16[4,64,1,640]{3,0,2,1:T(4,128)(2,1)}), bf16[4,64,1,640]{3,0,2,1:T(4,128)(2,1)S(1)}, u32[]{:S(2)}, u32[]{:S(2)}) async-start(bf16[4,64,1,640]{3,0,2,1:T(4,128)(2,1)} %copy.32), calls=%async_computation.1 | async-start | bytes 655360 | tf_op jit(solution)/shard_map/all_to_all | solution.py:55
  32.4 59.8 %copy-start.7 = (s32[256]{0:T(256)S(1)}, s32[256]{0:T(256)}, u32[]{:S(2)}) copy-start(s32[256]{0:T(256)} %param.18) | copy-start | bytes 3076
  56.1 29.5 %all-to-all-start.2 = ((bf16[4,64,1,640]{3,0,2,1:T(4,128)(2,1)}), bf16[4,64,1,640]{3,0,2,1:T(4,128)(2,1)S(1)}, u32[]{:S(2)}, u32[]{:S(2)}) async-start(bf16[4,64,1,640]{3,0,2,1:T(4,128)(2,1)} %copy.34), calls=%async_computation.2 | async-start | bytes 655360 | tf_op jit(solution)/shard_map/all_to_all | solution.py:56
  85.6 28.9 %all-to-all-start = ((bf16[4,64,1,640]{3,0,2,1:T(4,128)(2,1)}), bf16[4,64,1,640]{3,0,2,1:T(4,128)(2,1)S(1)}, u32[]{:S(2)}, u32[]{:S(2)}) async-start(bf16[4,64,1,640]{3,0,2,1:T(4,128)(2,1)} %copy.31), calls=%async_computation | async-start | bytes 655360 | tf_op jit(solution)/shard_map/all_to_all | solution.py:57
  92.1 162.6 %all-gather.5.cloned.1.call-start = ((), (), s32[]{:S(2)}) async-start(), calls=%async_computation.5 | async-start | bytes 2949120 | tf_op jit(solution)/shard_map/all_gather | solution.py:106
  217.2 10.9 copy-start.3
  229.4 102.6 %all-reduce.7.cloned.1.call-start = ((), (), s32[]{:S(2)}) async-start(), calls=%async_computation.3 | async-start | bytes 655360 | tf_op jit(solution)/shard_map/psum | solution.py:105
  231.8 380.5 %all-reduce.11.cloned.1.call-start = ((), (), s32[]{:S(2)}) async-start(), calls=%async_computation.7 | async-start | bytes 2621440
  257.7 74.3 %copy-start.8 = (bf16[2,320,640]{2,1,0:T(8,128)(2,1)S(1)}, bf16[2,320,640]{2,1,0:T(8,128)(2,1)}, u32[]{:S(2)}) copy-start(bf16[2,320,640]{2,1,0:T(8,128)(2,1)} %param.23) | copy-start | bytes 2457604
  334.7 418.3 %all-gather.7.cloned.1.call-start = ((), (), s32[]{:S(2)}) async-start(), calls=%async_computation.6 | async-start | bytes 2949120 | tf_op jit(solution)/shard_map/all_gather | solution.py:106
  725.0 105.2 %all-reduce.9.cloned.1.call-start = ((), (), s32[]{:S(2)}) async-start(), calls=%async_computation.4 | async-start | bytes 655360 | tf_op jit(solution)/shard_map/psum | solution.py:105
  727.3 382.7 %all-reduce.13.cloned.1.call-start = ((), (), s32[]{:S(2)}) async-start(), calls=%async_computation.8 | async-start | bytes 2621440
  755.9 74.3 %copy-start.9 = (bf16[2,320,640]{2,1,0:T(8,128)(2,1)S(1)}, bf16[2,320,640]{2,1,0:T(8,128)(2,1)}, u32[]{:S(2)}) copy-start(bf16[2,320,640]{2,1,0:T(8,128)(2,1)} %param.23) | copy-start | bytes 2457604
Sparse Core Ops, SparseCore 0:
  229.6 25.1 all-gather.4
  257.1 74.8 all-reduce.6
  335.7 276.5 all-reduce.10
  725.1 27.8 all-gather.6
  755.3 74.8 all-reduce.8
  833.4 276.5 all-reduce.12
